TPU v7x, 32 devices: a whole 2x2x4 slice. The times are simulated.
32 devices in a mesh: row: 16 (over z, x, core), grp: 2 (over y).
Axes of the slice: x: 2, y: 2, z: 4, core: 2. Of those that a mesh axis runs over, the one named last changes fastest.
Arguments:
- panel_rows: bfloat16 [16384, 1024], P(('row', 'grp')), may hold values from -300 to 300, as said below
- sign_bits: int32 [16384], P(('row', 'grp')), may hold values from 0 to 1
- sample_rows: int32 [8192], replicated, may hold values from 0 to 16383, as said below
Outputs:
- factor: float32 [1024, 1024], P('row', 'grp')
Inputs may be any that keep to these rules, and one draw needn't show every extreme that they name: `sample_rows`: distinct and ascending. Each aligned block of 512 rows (the rows of one device) holds at most 512 sampled rows, and at least a quarter of these blocks hold exactly 512. `panel_rows`: finite values.
All inputs are finite; a program needn't handle non-finite values.
Results may differ from a plain program's by a relative error of at most 0.0011.
Values may be sent and summed in bfloat16 or wider, within the bound.
No kernel may reach another device: no remote copies, remote signals or barrier semaphores. Data moves between devices by JAX's collectives and lax.ppermute only.
A program may use at most 64 MiB of HBM per device.

v0:
```python
import math
import jax
import jax.numpy as jnp
from jax import lax
from jax.sharding import PartitionSpec as P


def hadamard(table_size, dtype):
    row_ids = lax.broadcasted_iota(jnp.int32, (table_size, table_size), 0)
    col_ids = lax.broadcasted_iota(jnp.int32, (table_size, table_size), 1)
    shared = row_ids & col_ids
    parity = jnp.zeros((table_size, table_size), jnp.int32)
    for bit_pos in range(table_size.bit_length() - 1):
        parity = parity ^ shared >> bit_pos & 1
    return (1 - 2 * parity).astype(dtype)


def mix_lead(exchanged):
    lead_table = hadamard(exchanged.shape[0], jnp.float32)
    return jnp.einsum("ab,bic->aic", lead_table, exchanged, precision=lax.Precision.HIGHEST)


def mix_grp(exchanged):
    return lax.all_to_all(mix_lead(exchanged), "grp", split_axis=0, concat_axis=2, tiled=True)


def local(panel_rows, sign_bits, sample_rows):
    rows_dev, n_cols = panel_rows.shape
    n_row = lax.axis_size("row")
    n_grp = lax.axis_size("grp")
    flipped = panel_rows * (1 - 2 * sign_bits).astype(jnp.bfloat16)[:, None]
    local_table = hadamard(rows_dev, jnp.bfloat16)
    local_mix = jnp.dot(local_table, flipped, preferred_element_type=jnp.float32)
    grp_mixed = mix_grp(
        lax.all_to_all(local_mix[None], "grp", split_axis=2, concat_axis=0, tiled=True)
    )
    num_samples = sample_rows.shape[0]
    total_rows = rows_dev * n_row * n_grp
    norm_scale = 1.0 / math.sqrt(total_rows * num_samples)
    col_width = n_cols // n_grp
    col_start = lax.axis_index("grp") * col_width
    held = mix_lead(lax.all_to_all(grp_mixed, "row", split_axis=1, concat_axis=0, tiled=True))
    slice_width = held.shape[1]
    block_pos = lax.broadcasted_iota(jnp.int32, (n_row, slice_width), 0)
    inner_pos = lax.broadcasted_iota(jnp.int32, (n_row, slice_width), 1)
    held_ids = (
        (block_pos * n_grp + lax.axis_index("grp")) * rows_dev
        + lax.axis_index("row") * slice_width
        + inner_pos
    ).reshape(-1)
    found_pos = jnp.clip(jnp.searchsorted(sample_rows, held_ids), 0, num_samples - 1)
    is_sampled = jnp.take(sample_rows, found_pos) == held_ids
    held_flat = held.reshape(n_row * slice_width, n_cols)
    sketch_held = jnp.where(is_sampled[:, None], held_flat * norm_scale, 0.0).astype(jnp.bfloat16)
    shard_rows = lax.all_gather(sketch_held, "grp", axis=0, tiled=True)
    own_cols = lax.dynamic_slice_in_dim(shard_rows, col_start, col_width, 1)
    partial_value = lax.dot_general(
        shard_rows, own_cols, (((0,), (0,)), ((), ())), preferred_element_type=jnp.float32
    )
    gram_block = lax.psum_scatter(partial_value, "row", scatter_dimension=0, tiled=True)
    gathered = lax.all_gather(gram_block[None], ("row", "grp"), axis=0, tiled=True)
    gram_matrix = (
        gathered.reshape(n_row, n_grp, n_cols // n_row, col_width)
        .transpose(0, 2, 1, 3)
        .reshape(n_cols, n_cols)
    )
    lower_factor = jnp.linalg.cholesky(gram_matrix)
    row_width = n_cols // n_row
    return lax.dynamic_slice(
        lower_factor, (lax.axis_index("row") * row_width, col_start), (row_width, col_width)
    )


def solution(mesh):
    return jax.shard_map(
        local,
        mesh=mesh,
        in_specs=(P(("row", "grp"), None), P(("row", "grp")), P()),
        out_specs=P("row", "grp"),
        check_vma=False,
    )
```

profile of v0, /device:TPU:0, one launch (start us, length us, event | category | flops | bytes accessed | tf_op | source)
XLA Modules:
  0.0 551.8 jit_solution(12056221303512903881)
XLA Ops:
  7.2 4.2 convolution_bitcast_fusion
  11.4 4.6 copy.17
  16.0 28.9 %all_to_all.48 = f32[1,512,1024]{1,0,2:T(1,128)S(1)} all-to-all(f32[1,512,1024]{1,0,2:T(1,128)S(1)} %copy.17), channel_id=1, replica_groups=mesh['row'=16,'grp'=2] {'grp'}, dimensions={2} | all-to-all | bytes 4194304 | tf_op jit(solution)/shard_map/all_to_all | solution.py:35
  45.1 2.5 copy.26
  47.6 8.8 %fusion.3 = f32[2,512,512]{2,0,1:T(2,128)S(1)} fusion(f32[1,512,2,512]{3,2,1,0:T(2,128)} %copy.26), kind=kOutput, calls=%fused_computation.10 | convolution fusion | flops 12582936 | bytes 4194304 | tf_op jit(solution)/shard_map/ab,bic->aic/dot_general | solution.py:20
  56.4 1.7 copy.19
  58.1 3.8 all-to-all-start.1
  62.0 23.9 %all-to-all-done.1 = f32[2,512,512]{2,1,0:T(8,128)S(1)} async-done(((f32[2,512,512]{2,1,0:T(8,128)}), f32[2,512,512]{2,1,0:T(8,128)S(1)}, u32[]{:S(2)}, u32[]{:S(2)}) %all-to-all-start.1) | async-done | bytes 2097184 | tf_op jit(solution)/shard_map/all_to_all | solution.py:24
  85.9 1.8 copy.20
  87.7 6.1 %copy.21 = f32[1,512,1024]{2,0,1:T(1,128)} copy(f32[1,512,1024]{1,2,0:T(8,128)} %bitcast.76) | data formatting | bytes 4194304 | tf_op jit(solution)/shard_map/all_to_all | solution.py:24
  93.8 6.3 %all-to-all-start.2 = ((f32[1,512,1024]{2,0,1:T(1,128)}), f32[1,512,1024]{2,0,1:T(1,128)S(1)}, u32[]{:S(2)}, u32[]{:S(2)}) async-start(f32[1,512,1024]{2,0,1:T(1,128)} %copy.21), calls=%async_computation.2 | async-start | bytes 4194304 | tf_op jit(solution)/shard_map/all_to_all | solution.py:42
  100.7 47.4 %while.24 = (s32[]{:T(128)}, u32[512]{0:T(512)S(1)}, u32[512]{0:T(512)S(1)}, s32[8192]{0:T(1024)S(1)}, s32[16]{0:T(128)S(1)}, /*index=5*/s32[]{:T(128)}, s32[]{:T(128)}, s32[]{}) while((s32[]{:T(128)}, u32[512]{0:T(512)S(1)}, u32[512]{0:T(512)S(1)}, s32[8192]{0:T(1024)S(1)}, s32[16]{0:T(128)S(1)}, /*index=5*/s32[]{:T(128)}, ...), condition=%wide.region_1.2_spmd.clone, body=%wide.region_0.1_spmd.clone.sunk | while | flops 10756 | bytes 46253 | solution.py:51
  100.7 3.1 gather_fusion
  104.1 3.1 gather_fusion
  107.5 3.1 gather_fusion
  110.9 3.1 gather_fusion
  114.3 3.1 gather_fusion
  117.7 3.1 gather_fusion
  121.0 3.1 gather_fusion
  124.4 3.1 gather_fusion
  127.8 3.1 gather_fusion
  131.2 3.1 gather_fusion
  134.6 3.1 gather_fusion
  138.0 3.1 gather_fusion
  141.3 3.1 gather_fusion
  144.7 3.1 gather_fusion
  148.1 3.1 gather_fusion.1
  151.9 2.9 fusion.8
  155.4 1.3 fusion.5
  156.7 33.6 %all-gather.4.cloned.1.call-done = bf16[1024,1024]{1,0:T(8,128)(2,1)} async-done(((bf16[512,1024]{1,0:T(8,128)(2,1)}), bf16[1024,1024]{1,0:T(8,128)(2,1)}) %all-gather.4.cloned.1.call-update) | async-done | bytes 2097168 | tf_op jit(solution)/shard_map/all_gather | solution.py:55
  190.3 4.5 fusion.12
  194.9 61.9 %reduce-scatter.2.cloned.1.call-done = f32[64,512]{1,0:T(8,128)} async-done(((f32[1024,512]{1,0:T(8,128)}), f32[64,512]{1,0:T(8,128)}) %reduce-scatter.2.cloned.1.call-update) | async-done | bytes 131088 | tf_op jit(solution)/shard_map/reduce_scatter | solution.py:60
  256.8 63.6 %all-gather.6.cloned.1.call-done = f32[2048,512]{1,0:T(8,128)} async-done(((f32[64,512]{1,0:T(8,128)}), f32[2048,512]{1,0:T(8,128)}) %all-gather.6.cloned.1.call-update) | async-done | bytes 4194320 | tf_op jit(solution)/shard_map/all_gather | solution.py:61
  320.4 5.4 copy.24
  325.8 2.9 copy.29
  328.7 5.5 copy.25
  334.2 4.4 fusion.2
  338.7 1.9 copy-done.1
  340.6 11.7 %cholesky.223 = f32[128,128]{1,0:T(8,128)S(1)} custom-call(f32[128,128]{1,0:T(8,128)S(1)} %cholesky.580), custom_call_target="Cholesky" | custom-call | tf_op jit(solution)/shard_map/jit(cholesky)/cholesky | solution.py:67
  352.4 9.8 %custom-call.59 = f32[1,128,128]{1,2,0:T(8,128)S(1)} custom-call(f32[1,128,128]{2,1,0:T(8,128)S(1)} %get-tuple-element.125), custom_call_target="InvertDiagBlocksLowerTriangular" | custom-call | tf_op jit(solution)/shard_map/jit(cholesky)/cholesky | solution.py:67
  362.2 2.5 cholesky.255
  364.7 2.4 constant_dynamic-update-slice_fusion.5
  367.0 1.5 convolution_subtract_fusion
  368.6 11.9 %cholesky.244 = f32[128,128]{1,0:T(8,128)S(1)} custom-call(f32[128,128]{1,0:T(8,128)S(1)} %cholesky.584), custom_call_target="Cholesky" | custom-call | tf_op jit(solution)/shard_map/jit(cholesky)/cholesky | solution.py:67
  381.2 9.8 %custom-call.60 = f32[1,128,128]{1,2,0:T(8,128)S(1)} custom-call(f32[1,128,128]{2,1,0:T(8,128)S(1)} %get-tuple-element.122), custom_call_target="InvertDiagBlocksLowerTriangular" | custom-call | tf_op jit(solution)/shard_map/jit(cholesky)/cholesky | solution.py:67
  391.0 1.2 convolution_dynamic-update-slice_fusion
  392.2 2.1 convolution_subtract_fusion.1
  394.3 11.7 %cholesky.468 = f32[128,128]{1,0:T(8,128)S(1)} custom-call(f32[128,128]{1,0:T(8,128)S(1)} %cholesky.589), custom_call_target="Cholesky" | custom-call | tf_op jit(solution)/shard_map/jit(cholesky)/cholesky | solution.py:67
  407.3 9.8 %custom-call.61 = f32[1,128,128]{1,2,0:T(8,128)S(1)} custom-call(f32[1,128,128]{2,1,0:T(8,128)S(1)} %get-tuple-element.119), custom_call_target="InvertDiagBlocksLowerTriangular" | custom-call | tf_op jit(solution)/shard_map/jit(cholesky)/cholesky | solution.py:67
  418.3 2.3 convolution_subtract_fusion.2
  420.6 12.1 %cholesky.487 = f32[128,128]{1,0:T(8,128)S(1)} custom-call(f32[128,128]{1,0:T(8,128)S(1)} %cholesky.594), custom_call_target="Cholesky" | custom-call | tf_op jit(solution)/shard_map/jit(cholesky)/cholesky | solution.py:67
  434.0 9.8 %custom-call.62 = f32[1,128,128]{1,2,0:T(8,128)S(1)} custom-call(f32[1,128,128]{2,1,0:T(8,128)S(1)} %get-tuple-element.116), custom_call_target="InvertDiagBlocksLowerTriangular" | custom-call | tf_op jit(solution)/shard_map/jit(cholesky)/cholesky | solution.py:67
  444.9 2.3 convolution_subtract_fusion.3
  447.3 11.7 %cholesky.506 = f32[128,128]{1,0:T(8,128)S(1)} custom-call(f32[128,128]{1,0:T(8,128)S(1)} %cholesky.599), custom_call_target="Cholesky" | custom-call | tf_op jit(solution)/shard_map/jit(cholesky)/cholesky | solution.py:67
  460.3 9.9 %custom-call.63 = f32[1,128,128]{1,2,0:T(8,128)S(1)} custom-call(f32[1,128,128]{2,1,0:T(8,128)S(1)} %get-tuple-element.113), custom_call_target="InvertDiagBlocksLowerTriangular" | custom-call | tf_op jit(solution)/shard_map/jit(cholesky)/cholesky | solution.py:67
  471.2 2.3 convolution_subtract_fusion.4
  473.5 11.7 %cholesky.526 = f32[128,128]{1,0:T(8,128)S(1)} custom-call(f32[128,128]{1,0:T(8,128)S(1)} %cholesky.604), custom_call_target="Cholesky" | custom-call | tf_op jit(solution)/shard_map/jit(cholesky)/cholesky | solution.py:67
  486.5 9.8 %custom-call.64 = f32[1,128,128]{1,2,0:T(8,128)S(1)} custom-call(f32[1,128,128]{2,1,0:T(8,128)S(1)} %get-tuple-element.110), custom_call_target="InvertDiagBlocksLowerTriangular" | custom-call | tf_op jit(solution)/shard_map/jit(cholesky)/cholesky | solution.py:67
  497.3 2.0 convolution_subtract_fusion.5
  499.3 11.9 %cholesky.546 = f32[128,128]{1,0:T(8,128)S(1)} custom-call(f32[128,128]{1,0:T(8,128)S(1)} %cholesky.609), custom_call_target="Cholesky" | custom-call | tf_op jit(solution)/shard_map/jit(cholesky)/cholesky | solution.py:67
  512.5 9.8 %custom-call.65 = f32[1,128,128]{1,2,0:T(8,128)S(1)} custom-call(f32[1,128,128]{2,1,0:T(8,128)S(1)} %get-tuple-element.107), custom_call_target="InvertDiagBlocksLowerTriangular" | custom-call | tf_op jit(solution)/shard_map/jit(cholesky)/cholesky | solution.py:67
  523.1 1.8 convolution_subtract_fusion.6
  524.9 11.7 %cholesky.564 = f32[128,128]{1,0:T(8,128)S(1)} custom-call(f32[128,128]{1,0:T(8,128)S(1)} %convolution_subtract_fusion.6), custom_call_target="Cholesky" | custom-call | tf_op jit(solution)/shard_map/jit(cholesky)/cholesky | solution.py:67
  543.4 1.6 fusion.40
  (147 shorter events, 19.6 us)
Async XLA Ops:
  58.1 27.8 %all-to-all-start.1 = ((f32[2,512,512]{2,1,0:T(8,128)}), f32[2,512,512]{2,1,0:T(8,128)S(1)}, u32[]{:S(2)}, u32[]{:S(2)}) async-start(f32[2,512,512]{2,1,0:T(8,128)} %copy.19), calls=%async_computation.1 | async-start | bytes 4194304 | tf_op jit(solution)/shard_map/all_to_all | solution.py:24
  87.7 13.0 %copy-start = (s32[8192]{0:T(1024)S(1)}, s32[8192]{0:T(1024)}, u32[]{:S(2)}) copy-start(s32[8192]{0:T(1024)} %param.7) | copy-start | bytes 98308
  93.8 57.6 %all-to-all-start.2 = ((f32[1,512,1024]{2,0,1:T(1,128)}), f32[1,512,1024]{2,0,1:T(1,128)S(1)}, u32[]{:S(2)}, u32[]{:S(2)}) async-start(f32[1,512,1024]{2,0,1:T(1,128)} %copy.21), calls=%async_computation.2 | async-start | bytes 4194304 | tf_op jit(solution)/shard_map/all_to_all | solution.py:42
  100.2 90.1 %all-gather.4.cloned.1.call-start = ((), (), s32[]{:S(2)}) async-start(), calls=%async_computation.4 | async-start | bytes 3145728 | tf_op jit(solution)/shard_map/all_gather | solution.py:55
  156.6 100.1 %reduce-scatter.2.cloned.1.call-start = ((), (), s32[]{:S(2)}) async-start(), calls=%async_computation.5 | async-start | bytes 2228224 | tf_op jit(solution)/shard_map/reduce_scatter | solution.py:60
  194.8 125.5 %all-gather.6.cloned.1.call-start = ((), (), s32[]{:S(2)}) async-start(), calls=%async_computation.6 | async-start | bytes 4325376 | tf_op jit(solution)/shard_map/all_gather | solution.py:61
  338.7 1.9 copy-start.1
Sparse Core Ops, SparseCore 0:
  156.8 33.4 all-gather.3
  195.0 61.7 reduce-scatter.1
  259.7 60.6 all-gather.5
where the time goes:
time: 558 us; the launch traced here: 552 us
  waiting for transfers between devices  183 us (33%)
  other arithmetic  182 us (33%)
  local copies, waits for them, and re-layouts  84.7 us (15%)
  matrix products  43.5 us (8%)
  blocking collectives  28.9 us (5%)
  between operations  18.5 us (3%)
  starting transfers between devices  10.7 us (2%)
    another operation x30, other arithmetic, local(): lower_factor = jnp.linalg.cholesky(gram_matrix)  172 us
    all_gather x1, waiting for transfers between devices, local(): lax.all_gather(gram_block[None], ('row', 'grp'), axis=0, tiled=True)  63.6 us
    reduce_scatter x1, waiting for transfers between devices, local(): lax.psum_scatter(partial_value, 'row', scatter_dimension=0, tiled=True)  61.9 us
    gather x14, local copies, waits for them, and re-layouts, local(): jnp.searchsorted(sample_rows, held_ids)  44 us
    all_gather x1, waiting for transfers between devices, local(): shard_rows = lax.all_gather(sketch_held, 'grp', axis=0, tiled=True)  33.6 us
    all_to_all x1, blocking collectives, local(): lax.all_to_all(local_mix[None], 'grp', split_axis=2, concat_axis=0, tiled...  28.9 us
    all_to_all x1, waiting for transfers between devices, mix_grp(): lax.all_to_all(mix_lead(exchanged), 'grp', split_axis=0, concat_axis=2, t...  23.9 us
    another operation x14, matrix products, local(): lower_factor = jnp.linalg.cholesky(gram_matrix)  23.1 us
  transfers between devices with their start and end apart: 5, of which 4 were waited for; matrix products, arithmetic and copies ran while one was open for 9% of the time, Pallas kernels for 0%

commit v1 on v0

--- a/solution.py
+++ b/solution.py
@@ -1,8 +1,20 @@
+import functools
 import math
 import jax
 import jax.numpy as jnp
 from jax import lax
 from jax.sharding import PartitionSpec as P
+
+
+def positions_resolve(u_in, pos_dim, d0):
+    state_now = lax.axis_size("grp")
+    f_now = jnp.split(u_in, state_now, axis=pos_dim)
+    high = jnp.stack(f_now)
+    a_now = lax.all_to_all(high, axis_name="grp", split_axis=0, concat_axis=0)
+    return jnp.concatenate(a_now, d0)
+
+
+strips_all_make = functools.partial(positions_resolve, pos_dim=2, d0=0)
 
 
 def hadamard(table_size, dtype):
@@ -31,9 +43,7 @@
     flipped = panel_rows * (1 - 2 * sign_bits).astype(jnp.bfloat16)[:, None]
     local_table = hadamard(rows_dev, jnp.bfloat16)
     local_mix = jnp.dot(local_table, flipped, preferred_element_type=jnp.float32)
-    grp_mixed = mix_grp(
-        lax.all_to_all(local_mix[None], "grp", split_axis=2, concat_axis=0, tiled=True)
-    )
+    grp_mixed = mix_grp(strips_all_make(local_mix[None]))
     num_samples = sample_rows.shape[0]
     total_rows = rows_dev * n_row * n_grp
     norm_scale = 1.0 / math.sqrt(total_rows * num_samples)

time: 558 us -> 549 us (0.984)
  local copies, waits for them, and re-layouts: 84.7 us -> 77.6 us
where the time goes in v1:
time: 549 us; the launch traced here: 543 us
  waiting for transfers between devices  183 us (33%)
  other arithmetic  182 us (33%)
  local copies, waits for them, and re-layouts  77.6 us (14%)
  matrix products  41.4 us (8%)
  blocking collectives  28.9 us (5%)
  between operations  18.5 us (3%)
  starting transfers between devices  10.7 us (2%)
    another operation x30, other arithmetic, local(): lower_factor = jnp.linalg.cholesky(gram_matrix)  172 us
    all_gather x1, waiting for transfers between devices, local(): lax.all_gather(gram_block[None], ('row', 'grp'), axis=0, tiled=True)  63.5 us
    reduce_scatter x1, waiting for transfers between devices, local(): lax.psum_scatter(partial_value, 'row', scatter_dimension=0, tiled=True)  61.9 us
    gather x14, local copies, waits for them, and re-layouts, local(): jnp.searchsorted(sample_rows, held_ids)  44 us
    all_gather x1, waiting for transfers between devices, local(): shard_rows = lax.all_gather(sketch_held, 'grp', axis=0, tiled=True)  33.6 us
    all_to_all x1, blocking collectives, positions_resolve(): a_now = lax.all_to_all(high, axis_name='grp', split_axis=0, concat_axis=0)  28.9 us
    all_to_all x1, waiting for transfers between devices, mix_grp(): lax.all_to_all(mix_lead(exchanged), 'grp', split_axis=0, concat_axis=2, t...  23.9 us
    another operation x14, matrix products, local(): lower_factor = jnp.linalg.cholesky(gram_matrix)  23.1 us
  transfers between devices with their start and end apart: 5, of which 4 were waited for; matrix products, arithmetic and copies ran while one was open for 9% of the time, Pallas kernels for 0%

profile of v1, /device:TPU:0, one launch (start us, length us, event | category | flops | bytes accessed | tf_op | source)
XLA Modules:
  0.0 542.8 jit_solution(16340205755679342012)
XLA Ops:
  7.2 2.8 convolution_bitcast_fusion
  10.4 28.9 %all_to_all.35 = f32[2,1,512,512]{3,2,1,0:T(8,128)S(1)} all-to-all(f32[2,1,512,512]{3,2,1,0:T(8,128)S(1)} %pad_maximum_fusion), channel_id=1, replica_groups=mesh['row'=16,'grp'=2] {'grp'}, dimensions={0} | all-to-all | bytes 4194304 | tf_op jit(solution)/shard_map/all_to_all | solution.py:13
  39.3 8.1 %fusion.6 = f32[2,512,512]{2,0,1:T(2,128)S(1)} fusion(f32[2,512,512]{2,1,0:T(8,128)S(1)} %bitcast.74), kind=kOutput, calls=%fused_computation.15 | convolution fusion | flops 12582936 | bytes 4194304 | tf_op jit(solution)/shard_map/ab,bic->aic/dot_general | solution.py:32
  47.5 1.7 copy.19
  49.2 3.8 all-to-all-start.1
  53.0 23.9 %all-to-all-done.1 = f32[2,512,512]{2,1,0:T(8,128)S(1)} async-done(((f32[2,512,512]{2,1,0:T(8,128)}), f32[2,512,512]{2,1,0:T(8,128)S(1)}, u32[]{:S(2)}, u32[]{:S(2)}) %all-to-all-start.1) | async-done | bytes 2097184 | tf_op jit(solution)/shard_map/all_to_all | solution.py:36
  77.0 1.8 copy.20
  78.8 6.1 %copy.21 = f32[1,512,1024]{2,0,1:T(1,128)} copy(f32[1,512,1024]{1,2,0:T(8,128)} %bitcast.75) | data formatting | bytes 4194304 | tf_op jit(solution)/shard_map/all_to_all | solution.py:36
  84.9 6.3 %all-to-all-start.2 = ((f32[1,512,1024]{2,0,1:T(1,128)}), f32[1,512,1024]{2,0,1:T(1,128)S(1)}, u32[]{:S(2)}, u32[]{:S(2)}) async-start(f32[1,512,1024]{2,0,1:T(1,128)} %copy.21), calls=%async_computation.2 | async-start | bytes 4194304 | tf_op jit(solution)/shard_map/all_to_all | solution.py:52
  91.8 47.4 %while.24 = (s32[]{:T(128)}, u32[512]{0:T(512)S(1)}, u32[512]{0:T(512)S(1)}, s32[8192]{0:T(1024)S(1)}, s32[16]{0:T(128)S(1)}, /*index=5*/s32[]{:T(128)}, s32[]{:T(128)}, s32[]{}) while((s32[]{:T(128)}, u32[512]{0:T(512)S(1)}, u32[512]{0:T(512)S(1)}, s32[8192]{0:T(1024)S(1)}, s32[16]{0:T(128)S(1)}, /*index=5*/s32[]{:T(128)}, ...), condition=%wide.region_1.2_spmd.clone, body=%wide.region_0.1_spmd.clone.sunk | while | flops 10756 | bytes 46253 | solution.py:61
  91.8 3.1 gather_fusion
  95.2 3.1 gather_fusion
  98.6 3.1 gather_fusion
  102.0 3.1 gather_fusion
  105.3 3.1 gather_fusion
  108.7 3.1 gather_fusion
  112.1 3.1 gather_fusion
  115.5 3.1 gather_fusion
  118.9 3.1 gather_fusion
  122.3 3.1 gather_fusion
  125.6 3.1 gather_fusion
  129.0 3.1 gather_fusion
  132.4 3.1 gather_fusion
  135.8 3.1 gather_fusion
  139.2 3.1 gather_fusion.1
  143.0 2.9 fusion.8
  146.4 1.3 fusion.3
  147.8 33.6 %all-gather.4.cloned.1.call-done = bf16[1024,1024]{1,0:T(8,128)(2,1)} async-done(((bf16[512,1024]{1,0:T(8,128)(2,1)}), bf16[1024,1024]{1,0:T(8,128)(2,1)}) %all-gather.4.cloned.1.call-update) | async-done | bytes 2097168 | tf_op jit(solution)/shard_map/all_gather | solution.py:65
  181.3 4.5 fusion.12
  186.0 61.9 %reduce-scatter.2.cloned.1.call-done = f32[64,512]{1,0:T(8,128)} async-done(((f32[1024,512]{1,0:T(8,128)}), f32[64,512]{1,0:T(8,128)}) %reduce-scatter.2.cloned.1.call-update) | async-done | bytes 131088 | tf_op jit(solution)/shard_map/reduce_scatter | solution.py:70
  247.8 63.5 %all-gather.6.cloned.1.call-done = f32[2048,512]{1,0:T(8,128)} async-done(((f32[64,512]{1,0:T(8,128)}), f32[2048,512]{1,0:T(8,128)}) %all-gather.6.cloned.1.call-update) | async-done | bytes 4194320 | tf_op jit(solution)/shard_map/all_gather | solution.py:71
  311.4 5.4 %copy.24 = f32[16,2,64,512]{3,1,2,0:T(2,128)S(1)} copy(f32[16,2,64,512]{3,2,1,0:T(8,128)} %bitcast.77) | data formatting | bytes 8388608 | tf_op jit(solution)/shard_map/reshape | solution.py:73
  316.8 2.9 copy.27
  319.7 5.5 %copy.25 = f32[1024,1024]{0,1:T(8,128)} copy(f32[1024,1024]{1,0:T(8,128)} %bitcast.71) | data formatting | bytes 8388608 | tf_op jit(solution)/shard_map/reshape | solution.py:75
  325.2 4.4 fusion.2
  329.7 1.9 copy-done.1
  331.6 11.7 %cholesky.223 = f32[128,128]{1,0:T(8,128)S(1)} custom-call(f32[128,128]{1,0:T(8,128)S(1)} %cholesky.580), custom_call_target="Cholesky" | custom-call | tf_op jit(solution)/shard_map/jit(cholesky)/cholesky | solution.py:77
  343.4 9.8 %custom-call.59 = f32[1,128,128]{1,2,0:T(8,128)S(1)} custom-call(f32[1,128,128]{2,1,0:T(8,128)S(1)} %get-tuple-element.127), custom_call_target="InvertDiagBlocksLowerTriangular" | custom-call | tf_op jit(solution)/shard_map/jit(cholesky)/cholesky | solution.py:77
  353.2 2.5 cholesky.255
  355.7 2.4 constant_dynamic-update-slice_fusion.5
  358.1 1.5 convolution_subtract_fusion
  359.6 11.9 %cholesky.244 = f32[128,128]{1,0:T(8,128)S(1)} custom-call(f32[128,128]{1,0:T(8,128)S(1)} %cholesky.584), custom_call_target="Cholesky" | custom-call | tf_op jit(solution)/shard_map/jit(cholesky)/cholesky | solution.py:77
  372.2 9.8 %custom-call.60 = f32[1,128,128]{1,2,0:T(8,128)S(1)} custom-call(f32[1,128,128]{2,1,0:T(8,128)S(1)} %get-tuple-element.124), custom_call_target="InvertDiagBlocksLowerTriangular" | custom-call | tf_op jit(solution)/shard_map/jit(cholesky)/cholesky | solution.py:77
  382.0 1.2 convolution_dynamic-update-slice_fusion
  383.2 2.1 convolution_subtract_fusion.1
  385.3 11.7 %cholesky.468 = f32[128,128]{1,0:T(8,128)S(1)} custom-call(f32[128,128]{1,0:T(8,128)S(1)} %cholesky.589), custom_call_target="Cholesky" | custom-call | tf_op jit(solution)/shard_map/jit(cholesky)/cholesky | solution.py:77
  398.3 9.8 %custom-call.61 = f32[1,128,128]{1,2,0:T(8,128)S(1)} custom-call(f32[1,128,128]{2,1,0:T(8,128)S(1)} %get-tuple-element.121), custom_call_target="InvertDiagBlocksLowerTriangular" | custom-call | tf_op jit(solution)/shard_map/jit(cholesky)/cholesky | solution.py:77
  408.1 1.2 convolution_dynamic-update-slice_fusion.1
  409.3 2.3 convolution_subtract_fusion.2
  411.6 12.1 %cholesky.487 = f32[128,128]{1,0:T(8,128)S(1)} custom-call(f32[128,128]{1,0:T(8,128)S(1)} %cholesky.594), custom_call_target="Cholesky" | custom-call | tf_op jit(solution)/shard_map/jit(cholesky)/cholesky | solution.py:77
  425.0 9.8 %custom-call.62 = f32[1,128,128]{1,2,0:T(8,128)S(1)} custom-call(f32[1,128,128]{2,1,0:T(8,128)S(1)} %get-tuple-element.118), custom_call_target="InvertDiagBlocksLowerTriangular" | custom-call | tf_op jit(solution)/shard_map/jit(cholesky)/cholesky | solution.py:77
  434.8 1.1 convolution_dynamic-update-slice_fusion.2
  435.9 2.3 convolution_subtract_fusion.3
  438.3 11.7 %cholesky.506 = f32[128,128]{1,0:T(8,128)S(1)} custom-call(f32[128,128]{1,0:T(8,128)S(1)} %cholesky.599), custom_call_target="Cholesky" | custom-call | tf_op jit(solution)/shard_map/jit(cholesky)/cholesky | solution.py:77
  451.3 9.9 %custom-call.63 = f32[1,128,128]{1,2,0:T(8,128)S(1)} custom-call(f32[1,128,128]{2,1,0:T(8,128)S(1)} %get-tuple-element.115), custom_call_target="InvertDiagBlocksLowerTriangular" | custom-call | tf_op jit(solution)/shard_map/jit(cholesky)/cholesky | solution.py:77
  462.2 2.3 convolution_subtract_fusion.4
  464.5 11.7 %cholesky.526 = f32[128,128]{1,0:T(8,128)S(1)} custom-call(f32[128,128]{1,0:T(8,128)S(1)} %cholesky.604), custom_call_target="Cholesky" | custom-call | tf_op jit(solution)/shard_map/jit(cholesky)/cholesky | solution.py:77
  477.5 9.8 %custom-call.64 = f32[1,128,128]{1,2,0:T(8,128)S(1)} custom-call(f32[1,128,128]{2,1,0:T(8,128)S(1)} %get-tuple-element.112), custom_call_target="InvertDiagBlocksLowerTriangular" | custom-call | tf_op jit(solution)/shard_map/jit(cholesky)/cholesky | solution.py:77
  488.3 2.0 convolution_subtract_fusion.5
  490.3 11.9 %cholesky.546 = f32[128,128]{1,0:T(8,128)S(1)} custom-call(f32[128,128]{1,0:T(8,128)S(1)} %cholesky.609), custom_call_target="Cholesky" | custom-call | tf_op jit(solution)/shard_map/jit(cholesky)/cholesky | solution.py:77
  503.5 9.8 %custom-call.65 = f32[1,128,128]{1,2,0:T(8,128)S(1)} custom-call(f32[1,128,128]{2,1,0:T(8,128)S(1)} %get-tuple-element.109), custom_call_target="InvertDiagBlocksLowerTriangular" | custom-call | tf_op jit(solution)/shard_map/jit(cholesky)/cholesky | solution.py:77
  514.1 1.8 convolution_subtract_fusion.6
  515.9 11.7 %cholesky.564 = f32[128,128]{1,0:T(8,128)S(1)} custom-call(f32[128,128]{1,0:T(8,128)S(1)} %convolution_subtract_fusion.6), custom_call_target="Cholesky" | custom-call | tf_op jit(solution)/shard_map/jit(cholesky)/cholesky | solution.py:77
  534.5 1.6 fusion.40
  (146 shorter events, 17.5 us)
Async XLA Ops:
  49.2 27.8 %all-to-all-start.1 = ((f32[2,512,512]{2,1,0:T(8,128)}), f32[2,512,512]{2,1,0:T(8,128)S(1)}, u32[]{:S(2)}, u32[]{:S(2)}) async-start(f32[2,512,512]{2,1,0:T(8,128)} %copy.19), calls=%async_computation.1 | async-start | bytes 4194304 | tf_op jit(solution)/shard_map/all_to_all | solution.py:36
  78.8 13.0 %copy-start = (s32[8192]{0:T(1024)S(1)}, s32[8192]{0:T(1024)}, u32[]{:S(2)}) copy-start(s32[8192]{0:T(1024)} %param.7) | copy-start | bytes 98308
  84.9 57.6 %all-to-all-start.2 = ((f32[1,512,1024]{2,0,1:T(1,128)}), f32[1,512,1024]{2,0,1:T(1,128)S(1)}, u32[]{:S(2)}, u32[]{:S(2)}) async-start(f32[1,512,1024]{2,0,1:T(1,128)} %copy.21), calls=%async_computation.2 | async-start | bytes 4194304 | tf_op jit(solution)/shard_map/all_to_all | solution.py:52
  91.2 90.1 %all-gather.4.cloned.1.call-start = ((), (), s32[]{:S(2)}) async-start(), calls=%async_computation.4 | async-start | bytes 3145728 | tf_op jit(solution)/shard_map/all_gather | solution.py:65
  147.7 100.1 %reduce-scatter.2.cloned.1.call-start = ((), (), s32[]{:S(2)}) async-start(), calls=%async_computation.5 | async-start | bytes 2228224 | tf_op jit(solution)/shard_map/reduce_scatter | solution.py:70
  185.9 125.5 %all-gather.6.cloned.1.call-start = ((), (), s32[]{:S(2)}) async-start(), calls=%async_computation.6 | async-start | bytes 4325376 | tf_op jit(solution)/shard_map/all_gather | solution.py:71
  329.7 1.9 copy-start.1
Sparse Core Ops, SparseCore 0:
  147.8 33.4 all-gather.3
  186.0 61.7 reduce-scatter.1
  250.7 60.6 all-gather.5
